TPU v7x, 512 devices: a whole 4x4x16 slice. The times are simulated.
512 devices in a mesh: slab: 128 (over x, z, core), sub: 4 (over y).
Axes of the slice: x: 4, y: 4, z: 16, core: 2. Of those that a mesh axis runs over, the one named last changes fastest.
Arguments:
- ensemble: float32 [2, 15, 80, 65536], P(None, None, None, ('slab', 'sub')), may hold values from -6 to 6
- obs_value: float32 [2, 256], replicated, may hold values from -6 to 6
- obs_var: float32 [2, 256], replicated, may hold values from 0.5 to 4
- obs_owner: int32 [2, 256, 1], replicated, may hold values from 0 to 127; in each aligned block of 256 rows (0 to 255, 256 to 511, ..., all dimensions but the last counted through in order) at most 8 rows name the same one
- obs_column: int32 [2, 256], replicated, may hold values from 0 to 511
- home_block: int32 [2, 256], replicated, may hold values from -1 to 1
- batch_order: int32 [2], replicated, may hold values from 0 to 1, each once
Outputs:
- analysis: float32 [2, 15, 80, 65536], P(None, None, None, ('slab', 'sub'))
- assimilated_priors: float32 [2, 256, 160], replicated
Inputs may be any that keep to these rules, and one draw needn't show every extreme that they name: `obs_owner`: in each batch no slab owns more than 8 observations; in some batch one slab owns exactly 8. `batch_order`: each batch appears once.
All inputs are finite; a program needn't handle non-finite values.
Results may differ from a plain program's by a relative error of at most 0.00012.
Values sent between devices are 32-bit elements; how exact they have to be, the bound alone decides.
A program may use at most 64 MiB of HBM per device.

v0:
```python
import jax
import jax.numpy as jnp
from jax import lax
from jax.sharding import PartitionSpec as P

BANDS = 2
BLK = 16
BATCHES = 2
CAP = 8
HIGHEST = lax.Precision.HIGHEST


def gc_weight(first, second, nblocks, length):
    block_gap = jnp.abs(first - second)
    block_gap = jnp.minimum(block_gap, nblocks - block_gap)
    scaled_gap = block_gap.astype(jnp.float32) / length
    near_part = (
        ((-0.25 * scaled_gap + 0.5) * scaled_gap + 0.625) * scaled_gap**3
        - 5.0 / 3.0 * scaled_gap**2
        + 1.0
    )
    floored = jnp.maximum(scaled_gap, 1.0)
    far_part = (
        (
            (((scaled_gap / 12.0 - 0.5) * scaled_gap + 0.625) * scaled_gap + 5.0 / 3.0) * scaled_gap
            - 5.0
        )
        * scaled_gap
        + 4.0
        - 2.0 / (3.0 * floored)
    )
    return jnp.where(scaled_gap <= 1.0, near_part, jnp.where(scaled_gap < 2.0, far_part, 0.0))


def obs_statistics(current, values, variances, members):
    banded = current.reshape(current.shape[0], BANDS, members)
    whole_obs = jnp.sum(banded, axis=1)
    centre = jnp.mean(whole_obs, axis=1, keepdims=True)
    spread = jnp.sum((whole_obs - centre) ** 2, axis=1) / (members - 1) + 1e-06
    post_var = 1.0 / (1.0 / spread + 1.0 / variances)
    post_mean = post_var * (centre[:, 0] / spread + values / variances)
    increments = (post_mean - centre[:, 0])[:, None] + (jnp.sqrt(post_var / spread) - 1.0)[
        :, None
    ] * (whole_obs - centre)
    deviations = banded - jnp.mean(banded, axis=2, keepdims=True)
    return (deviations, spread, increments)


def update_pool(pool, pool_homes, deviations, spread, increments, obs_homes, nblocks, decays):
    members = deviations.shape[2]
    banded = pool.reshape(pool.shape[0], BANDS, members)
    new_bands = []
    for band_no in range(BANDS):
        pool_band = banded[:, band_no, :]
        pool_dev = pool_band - jnp.mean(pool_band, axis=1, keepdims=True)
        weights = (
            gc_weight(pool_homes[:, None], obs_homes[None, :], nblocks, decays[band_no])
            / ((members - 1) * spread)[None, :]
        )
        crossed = jnp.einsum("pm,km->pk", pool_dev, deviations[:, band_no, :], precision=HIGHEST)
        change = jnp.einsum("pk,km->pm", crossed * weights, increments, precision=HIGHEST)
        new_bands.append(pool_band + change)
    return jnp.stack(new_bands, axis=1).reshape(pool.shape)


def update_state(
    ensemble, my_cols, deviations, spread, increments, obs_homes, valid, nblocks, decays
):
    members = ensemble.shape[2]
    new_bands = []
    for band_no in range(BANDS):
        band_layer = ensemble[band_no]
        layer_dev = band_layer - jnp.mean(band_layer, axis=1, keepdims=True)
        obs_dev = deviations[:, band_no, :]
        weights = (
            gc_weight((my_cols // BLK)[:, None], obs_homes[None, :], nblocks, decays[band_no])
            / ((members - 1) * spread)[None, :]
        )
        weights = jnp.where(valid[None, :], weights, 0.0)
        crossed = jnp.einsum("lmc,km->lck", layer_dev, obs_dev, precision=HIGHEST)
        change = jnp.einsum("lck,km->lmc", crossed * weights[None], increments, precision=HIGHEST)
        new_bands.append(band_layer + change)
    return jnp.stack(new_bands, axis=0)


def slot_table(owners, slot_rank, slab_number, capacity):
    obs_count = owners.shape[1]
    matches = (owners == slab_number)[:, None, :] & (
        slot_rank[:, None, :] == jnp.arange(capacity, dtype=jnp.int32)[None, :, None]
    )
    slot_obs = jnp.sum(
        jnp.where(matches, jnp.arange(obs_count, dtype=jnp.int32)[None, None, :], 0), axis=2
    )
    slot_valid = jnp.any(matches, axis=2)
    return (slot_obs, slot_valid)


def per_device(ensemble, obs_value, obs_var, obs_owner, obs_column, home_block, batch_order):
    members = ensemble.shape[2]
    levels_count = ensemble.shape[1]
    cols_dev = ensemble.shape[3]
    slab_count = lax.axis_size("slab")
    sub_count = lax.axis_size("sub")
    slab_index = lax.axis_index("slab")
    sub_index = lax.axis_index("sub")
    capacity = CAP
    cols_slab = cols_dev * sub_count
    nblocks = cols_slab * slab_count // BLK
    span_broad = cols_slab // (4 * BLK)
    span_narrow = max(span_broad // 4, 1)
    decays = (float(span_broad), float(span_narrow))
    assert 2 * span_broad + 1 <= cols_slab // BLK and slab_count >= 3
    owners = obs_owner[:, :, 0]
    obs_home = jnp.mod((owners * cols_slab + obs_column) // BLK + home_block, nblocks)
    onehot = (owners[:, :, None] == jnp.arange(slab_count, dtype=jnp.int32)[None, None, :]).astype(
        jnp.int32
    )
    running = jnp.cumsum(onehot, axis=1) - 1
    slot_rank = jnp.sum(onehot * running, axis=2)
    slot_global = owners * capacity + slot_rank
    slot_obs, slot_valid = slot_table(owners, slot_rank, slab_index, capacity)
    slot_column = jnp.take_along_axis(obs_column, slot_obs, axis=1)
    slot_level = slot_obs % levels_count
    holder = slot_column // cols_dev
    local_col = slot_column % cols_dev
    picked = ensemble[:, slot_level, :, local_col]
    retain = slot_valid & (holder == sub_index)
    picked = jnp.where(retain[:, :, None, None], picked, 0.0).reshape(
        BATCHES, capacity, BANDS * members
    )
    slab_slots = jnp.sum(lax.all_gather(picked, "sub", axis=0), axis=0)
    gathered = lax.all_gather(slab_slots, "slab", axis=1, tiled=True)
    priors = jnp.take_along_axis(gathered, slot_global[:, :, None], axis=1)
    first, second = (batch_order[0], batch_order[1])
    y0 = priors[first]
    stats0 = obs_statistics(y0, obs_value[first], obs_var[first], members)
    y1 = update_pool(priors[second], obs_home[second], *stats0, obs_home[first], nblocks, decays)
    stats1 = obs_statistics(y1, obs_value[second], obs_var[second], members)
    recorded = jnp.zeros_like(priors).at[first].set(y0).at[second].set(y1)
    my_cols = (slab_index * sub_count + sub_index) * cols_dev + jnp.arange(
        cols_dev, dtype=jnp.int32
    )
    near = [jnp.mod(slab_index + d, slab_count) for d in (-1, 0, 1)]
    for batch_id, stats in ((first, stats0), (second, stats1)):
        deviations, spread, increments = stats
        b_owners = lax.dynamic_index_in_dim(owners, batch_id, keepdims=True)
        b_rank = lax.dynamic_index_in_dim(slot_rank, batch_id, keepdims=True)
        tables = [slot_table(b_owners, b_rank, n, capacity) for n in near]
        idx = jnp.concatenate([t[0][0] for t in tables])
        valid = jnp.concatenate([t[1][0] for t in tables])
        ensemble = update_state(
            ensemble,
            my_cols,
            deviations[idx],
            spread[idx],
            increments[idx],
            obs_home[batch_id][idx],
            valid,
            nblocks,
            decays,
        )
    return (ensemble, recorded)


def solution(mesh):
    placed = (P(None, None, None, ("slab", "sub")), P(), P(), P(), P(), P(), P())
    return jax.shard_map(
        per_device,
        mesh=mesh,
        in_specs=placed,
        out_specs=(P(None, None, None, ("slab", "sub")), P()),
        check_vma=False,
    )
```

profile of v0, /device:TPU:1, one launch (start us, length us, event | category | flops | bytes accessed | tf_op | source)
XLA Modules:
  0.0 194.4 jit_solution(9131951338326680747)
XLA Ops:
  7.2 0.7 copy.71
  7.9 0.7 broadcast_compare_fusion
  8.6 0.8 copy.45
  10.7 0.7 gather_fusion.9
  11.7 1.0 copy.47
  12.8 0.6 gather_fusion
  13.6 10.3 %all_gather.6 = f32[4,2,8,160]{3,2,1,0:T(8,128)S(1)} all-gather(f32[1,2,8,160]{3,2,1,0:T(8,128)S(1)} %broadcast_select_fusion.1), channel_id=1, replica_groups=mesh['slab'=128,'sub'=4] {'sub'}, dimensions={0}, use_global_device_ids=true | all-gather | bytes 51200 | tf_op jit(solution)/shard_map/all_gather | solution.py:131
  23.9 0.6 reduce_sum.213
  24.6 0.6 fusion.104
  29.5 0.7 gather_fusion.3
  30.2 0.7 gather_fusion.7
  31.4 0.7 and_reduce_fusion
  32.2 132.7 %all-gather.2.cloned.1.call-done = f32[2,1024,160]{2,1,0:T(8,128)} async-done(((f32[2,8,160]{2,1,0:T(8,128)}), f32[2,1024,160]{2,1,0:T(8,128)}) %all-gather.2.cloned.1.call-update) | async-done | bytes 1310736 | tf_op jit(solution)/shard_map/all_gather | solution.py:132
  164.9 6.2 %gather_fusion.10 = f32[512,160]{1,0:T(8,128)S(1)} fusion(f32[2,1024,160]{2,1,0:T(8,128)} %all-gather.2.cloned.1.call-done, s32[512]{0:T(512)S(1)} %bitcast.158), kind=kCustom, calls=%fused_computation.10 | custom fusion | bytes 659456 | tf_op jit(solution)/shard_map/jit(take_along_axis)/gather | solution.py:133
  171.4 0.7 select_dynamic-update-slice_fusion
  172.9 0.6 gather_fusion.2
  174.1 0.6 gather_fusion.1
  174.7 0.8 convolution_multiply_fusion
  175.8 0.7 gather_fusion.4
  176.5 0.8 convolution_multiply_fusion.1
  177.8 0.7 gather_fusion.8
  179.2 0.7 fusion.106
  180.1 0.6 gather_fusion.6
  180.8 0.6 gather_fusion.5
  181.9 0.7 fusion.105
  182.6 0.5 convolution_multiply_fusion.4
  183.1 0.7 fusion.4
  183.8 0.5 convolution_multiply_fusion.2
  184.3 0.7 fusion.1
  185.0 1.2 pad_maximum_fusion
  186.2 0.6 constant_dynamic-update-slice_fusion
  186.8 0.7 copy-done.2
  (93 shorter events, 6.7 us)
Async XLA Ops:
  7.2 3.6 %copy-start = (s32[2,256]{1,0:T(2,128)S(1)}, s32[2,256]{1,0:T(2,128)}, u32[]{:S(2)}) copy-start(s32[2,256]{1,0:T(2,128)} %param.15) | copy-start | bytes 6148
  7.2 157.8 %all-gather.2.cloned.1.call-start = ((), (), s32[]{:S(2)}) async-start(), calls=%async_computation | async-start | bytes 2113536 | tf_op jit(solution)/shard_map/all_gather | solution.py:132
  9.9 1.8 copy-start.1
  11.7 12.8 %copy-start.4 = (s32[2]{0:T(128)S(1)}, s32[2]{0:T(128)}, u32[]{:S(2)}) copy-start(s32[2]{0:T(128)} %param.17) | copy-start | bytes 28
  11.7 16.0 %copy-start.3 = (s32[2,256,1]{1,2,0:T(1,128)S(1)}, s32[2,256,1]{1,2,0:T(1,128)}, u32[]{:S(2)}) copy-start(s32[2,256,1]{1,2,0:T(1,128)} %param.14) | copy-start | bytes 6148
  11.7 17.8 %copy-start.5 = (s32[2,256]{1,0:T(2,128)S(1)}, s32[2,256]{1,0:T(2,128)}, u32[]{:S(2)}) copy-start(s32[2,256]{1,0:T(2,128)} %param.16) | copy-start | bytes 6148
  12.8 18.6 %copy-start.6 = (f32[2,256]{1,0:T(2,128)S(1)}, f32[2,256]{1,0:T(2,128)}, u32[]{:S(2)}) copy-start(f32[2,256]{1,0:T(2,128)} %param.12) | copy-start | bytes 6148
  12.8 18.5 %copy-start.7 = (f32[2,256]{1,0:T(2,128)S(1)}, f32[2,256]{1,0:T(2,128)}, u32[]{:S(2)}) copy-start(f32[2,256]{1,0:T(2,128)} %param.13) | copy-start | bytes 6148
  12.8 18.6 %copy-start.8 = (s32[3]{0:T(128)S(1)}, s32[3]{0:T(128)}, u32[]{:S(2)}) copy-start(s32[3]{0:T(128)} %constant.306.clone.1) | copy-start | bytes 40
  186.8 0.7 copy-start.2
Sparse Core Ops, SparseCore 0:
  24.7 140.2 all-gather.1
where the time goes:
time: 195 us; the launch traced here: 194 us
  waiting for transfers between devices  133 us (68%)
  between operations  18.4 us (9%)
  local copies, waits for them, and re-layouts  18 us (9%)
  blocking collectives  10.3 us (5%)
  other arithmetic  7.86 us (4%)
  matrix products  7.03 us (4%)
    all_gather x1, waiting for transfers between devices, per_device(): gathered = lax.all_gather(slab_slots, 'slab', axis=1, tiled=True)  133 us
    all_gather x1, blocking collectives, per_device(): slab_slots = jnp.sum(lax.all_gather(picked, 'sub', axis=0), axis=0)  10.3 us
    gather x2, local copies, waits for them, and re-layouts, per_device(): priors = jnp.take_along_axis(gathered, slot_global[:, :, None], axis=1)  6.32 us
  transfers between devices with their start and end apart: 1, of which 1 were waited for; matrix products, arithmetic and copies ran while one was open for 2% of the time, Pallas kernels for 0%

commit v1 on v0

--- a/solution.py
+++ b/solution.py
@@ -129,7 +129,10 @@
         BATCHES, capacity, BANDS * members
     )
     slab_slots = jnp.sum(lax.all_gather(picked, "sub", axis=0), axis=0)
-    gathered = lax.all_gather(slab_slots, "slab", axis=1, tiled=True)
+    size = lax.axis_size("slab")
+    blocks = jnp.stack([slab_slots for _ in range(size)])
+    blocks = lax.all_to_all(blocks, "slab", split_axis=0, concat_axis=0)
+    gathered = jnp.concatenate(blocks, axis=1)
     priors = jnp.take_along_axis(gathered, slot_global[:, :, None], axis=1)
     first, second = (batch_order[0], batch_order[1])
     y0 = priors[first]

time: 195 us -> 167 us (0.86)
  waiting for transfers between devices: 133 us -> 90.9 us
  starting transfers between devices: 0.04 us -> 23.1 us
  between operations: 18.4 us -> 5.12 us
  local copies, waits for them, and re-layouts: 18 us -> 22.6 us
    all_gather x1 -> x0, waiting for transfers between devices: 133 us -> none  [per_device(): gathered = lax.all_gather(slab_slots, 'slab', axis=1, tiled=True)]
    all_to_all x0 -> x1, waiting for transfers between devices: none -> 90.9 us  [per_device(): blocks = lax.all_to_all(blocks, 'slab', split_axis=0, concat_axis=0)]
    all_to_all x0 -> x1, starting transfers between devices: none -> 23.1 us  [per_device(): blocks = lax.all_to_all(blocks, 'slab', split_axis=0, concat_axis=0)]
where the time goes in v1:
time: 167 us; the launch traced here: 166 us
  waiting for transfers between devices  90.9 us (54%)
  starting transfers between devices  23.1 us (14%)
  local copies, waits for them, and re-layouts  22.6 us (14%)
  blocking collectives  10.3 us (6%)
  other arithmetic  7.38 us (4%)
  matrix products  7.01 us (4%)
  between operations  5.12 us (3%)
    all_to_all x1, waiting for transfers between devices, per_device(): blocks = lax.all_to_all(blocks, 'slab', split_axis=0, concat_axis=0)  90.9 us
    all_to_all x1, starting transfers between devices, per_device(): blocks = lax.all_to_all(blocks, 'slab', split_axis=0, concat_axis=0)  23.1 us
    all_gather x1, blocking collectives, per_device(): slab_slots = jnp.sum(lax.all_gather(picked, 'sub', axis=0), axis=0)  10.3 us
    gather x2, local copies, waits for them, and re-layouts, per_device(): priors = jnp.take_along_axis(gathered, slot_global[:, :, None], axis=1)  7.59 us
  transfers between devices with their start and end apart: 1, of which 1 were waited for; matrix products, arithmetic and copies ran while one was open for 2% of the time, Pallas kernels for 0%

profile of v1, /device:TPU:1, one launch (start us, length us, event | category | flops | bytes accessed | tf_op | source)
XLA Modules:
  0.0 166.3 jit_solution(6122889330911309577)
XLA Ops:
  0.6 0.7 copy.74
  1.3 0.7 broadcast_compare_fusion
  2.0 0.8 copy.46
  4.2 0.7 gather_fusion.9
  5.1 1.0 copy.48
  6.2 0.6 gather_fusion
  7.0 10.3 %all_gather.3 = f32[4,2,8,160]{3,2,1,0:T(8,128)S(1)} all-gather(f32[1,2,8,160]{3,2,1,0:T(8,128)S(1)} %broadcast_select_fusion.1), channel_id=1, replica_groups=mesh['slab'=128,'sub'=4] {'sub'}, dimensions={0}, use_global_device_ids=true | all-gather | bytes 51200 | tf_op jit(solution)/shard_map/all_gather | solution.py:131
  17.3 1.6 stack.14
  18.8 23.1 %all-to-all-start = ((f32[128,2,8,160]{3,2,1,0:T(8,128)}), f32[128,2,8,160]{3,2,1,0:T(8,128)}, u32[]{:S(2)}, u32[]{:S(2)}) async-start(f32[128,2,8,160]{3,2,1,0:T(8,128)} %stack.14), calls=%async_computation | async-start | bytes 4194304 | tf_op jit(solution)/shard_map/all_to_all | solution.py:134
  42.0 0.6 fusion.104
  47.0 0.7 gather_fusion.3
  47.8 0.7 gather_fusion.7
  48.9 0.8 and_reduce_fusion
  49.8 90.9 %all-to-all-done = f32[128,2,8,160]{3,2,1,0:T(8,128)} async-done(((f32[128,2,8,160]{3,2,1,0:T(8,128)}), f32[128,2,8,160]{3,2,1,0:T(8,128)}, u32[]{:S(2)}, u32[]{:S(2)}) %all-to-all-start) | async-done | bytes 1310752 | tf_op jit(solution)/shard_map/all_to_all | solution.py:134
  140.7 1.7 %copy_bitcast_fusion = f32[2,1024,160]{2,1,0:T(8,128)S(1)} fusion(f32[128,2,8,160]{3,2,1,0:T(8,128)} %all-to-all-done), kind=kLoop, calls=%fused_computation.11 | loop fusion | bytes 2621440 | tf_op jit(solution)/shard_map/reshape | solution.py:135
  142.4 6.4 %gather_fusion.10 = f32[512,160]{1,0:T(8,128)} fusion(f32[2,1024,160]{2,1,0:T(8,128)S(1)} %copy_bitcast_fusion, s32[512]{0:T(512)S(1)} %bitcast.163), kind=kCustom, calls=%fused_computation.10 | custom fusion | bytes 659456 | tf_op jit(solution)/shard_map/jit(take_along_axis)/gather | solution.py:136
  148.8 1.2 copy.50
  150.1 0.7 select_dynamic-update-slice_fusion
  151.7 0.6 gather_fusion.2
  153.4 0.8 convolution_multiply_fusion
  154.6 0.7 gather_fusion.4
  155.3 0.8 convolution_multiply_fusion.1
  156.6 0.7 gather_fusion.8
  158.0 0.7 fusion.106
  158.9 0.6 gather_fusion.6
  159.6 0.6 gather_fusion.5
  160.7 0.7 fusion.105
  161.9 0.7 fusion.4
  163.1 0.7 fusion.1
  163.8 1.2 pad_maximum_fusion
  164.9 0.6 constant_dynamic-update-slice_fusion
  165.6 0.7 copy-done.2
  (94 shorter events, 8.0 us)
Async XLA Ops:
  0.6 3.5 %copy-start = (s32[2,256]{1,0:T(2,128)S(1)}, s32[2,256]{1,0:T(2,128)}, u32[]{:S(2)}) copy-start(s32[2,256]{1,0:T(2,128)} %param.15) | copy-start | bytes 6148
  3.3 1.8 %copy-start.1 = (f32[2,15,80,128]{3,2,1,0:T(8,128)S(1)}, f32[2,15,80,128]{3,2,1,0:T(8,128)}, u32[]{:S(2)}) copy-start(f32[2,15,80,128]{3,2,1,0:T(8,128)} %param.11) | copy-start | bytes 3686404
  18.8 23.1 %copy-start.4 = (s32[2]{0:T(128)S(1)}, s32[2]{0:T(128)}, u32[]{:S(2)}) copy-start(s32[2]{0:T(128)} %param.17) | copy-start | bytes 28
  18.8 26.3 %copy-start.3 = (s32[2,256,1]{1,2,0:T(1,128)S(1)}, s32[2,256,1]{1,2,0:T(1,128)}, u32[]{:S(2)}) copy-start(s32[2,256,1]{1,2,0:T(1,128)} %param.14) | copy-start | bytes 6148
  18.8 28.1 %copy-start.5 = (s32[2,256]{1,0:T(2,128)S(1)}, s32[2,256]{1,0:T(2,128)}, u32[]{:S(2)}) copy-start(s32[2,256]{1,0:T(2,128)} %param.16) | copy-start | bytes 6148
  18.8 121.8 %all-to-all-start = ((f32[128,2,8,160]{3,2,1,0:T(8,128)}), f32[128,2,8,160]{3,2,1,0:T(8,128)}, u32[]{:S(2)}, u32[]{:S(2)}) async-start(f32[128,2,8,160]{3,2,1,0:T(8,128)} %stack.14), calls=%async_computation | async-start | bytes 4194304 | tf_op jit(solution)/shard_map/all_to_all | solution.py:134
  41.9 6.9 %copy-start.6 = (f32[2,256]{1,0:T(2,128)S(1)}, f32[2,256]{1,0:T(2,128)}, u32[]{:S(2)}) copy-start(f32[2,256]{1,0:T(2,128)} %param.12) | copy-start | bytes 6148
  41.9 6.9 %copy-start.7 = (f32[2,256]{1,0:T(2,128)S(1)}, f32[2,256]{1,0:T(2,128)}, u32[]{:S(2)}) copy-start(f32[2,256]{1,0:T(2,128)} %param.13) | copy-start | bytes 6148
  41.9 6.9 %copy-start.8 = (s32[3]{0:T(128)S(1)}, s32[3]{0:T(128)}, u32[]{:S(2)}) copy-start(s32[3]{0:T(128)} %constant.306.clone.1) | copy-start | bytes 40
  165.6 0.7 copy-start.2
